TPU v7x, 512 devices: a whole 4x4x16 slice. The times are simulated.
512 devices in a mesh: prow: 32 (over y_lo, z), pcol: 16 (over y_hi, x, core).
Axes of the slice: x: 4, y: 4 (y_hi: 2, y_lo: 2; y = y_hi * 2 + y_lo), z: 16, core: 2. Of those that a mesh axis runs over, the one named last changes fastest.
Arguments:
- slab: bfloat16 [16384, 4096], P('prow', 'pcol'), may hold values from -6 to 6
- panels: bfloat16 [1, 16384, 512], P(None, 'prow', 'pcol'), may hold values from -0.25 to 0.25
- pivots: int32 [1, 512], replicated, may hold values from 0 to 16383, as said below
Outputs:
- factored_slab: bfloat16 [16384, 4096], P('prow', 'pcol')
Inputs may be any that keep to these rules, and one draw needn't show every extreme that they name: pivots[j, k] lies between j * 512 + k and 16383.
All inputs are finite; a program needn't handle non-finite values.
Results may differ from a plain program's by a relative error of at most 0.0041.
Values may be sent and summed in bfloat16 or wider, within the bound.
A program may use at most 64 MiB of HBM per device.

v0:
```python
import jax
import jax.numpy as jnp
from jax import lax
from jax.sharding import PartitionSpec as P

BLOCK_COLS = 512


def picked_2(x, axis, root):
    return lax.dynamic_index_in_dim(lax.all_gather(x, axis), root, 0, keepdims=False)


def cut_along(x, dim, size):
    before, after = (x.shape[:dim], x.shape[dim + 1 :])
    return jnp.moveaxis(x.reshape(*before, size, -1, *after), dim, 0)


def sum_at_owner(x, axis, dim):
    pieces = cut_along(x, dim, lax.axis_size(axis))
    arrived = lax.all_to_all(pieces, axis, split_axis=0, concat_axis=0, tiled=True)
    return arrived.astype(jnp.float32).sum(axis=0)


def swap_sources(pivot_row, top_row):
    count = pivot_row.shape[0]
    steps = jnp.arange(count, dtype=jnp.int32)
    relative = pivot_row - top_row
    earlier = steps[:, None] < steps[None, :]
    hit = (relative[:, None] == steps[None, :]) & earlier
    parent = jnp.max(jnp.where(hit, steps[:, None], -1), axis=0)
    pointer = jnp.where(parent >= 0, parent, steps)
    for turn in range(count.bit_length()):
        pointer = jnp.take(pointer, pointer)
    same = (pivot_row[:, None] == pivot_row[None, :]) & earlier
    latest = jnp.max(jnp.where(same, steps[:, None], -1), axis=0)
    top_source = jnp.where(
        latest >= 0, top_row + jnp.take(pointer, jnp.clip(latest, 0, count - 1)), pivot_row
    )
    return (pointer, top_source)


def triangle(diagonal, right_side):
    return jax.scipy.linalg.solve_triangular(
        diagonal, right_side, lower=True, unit_diagonal=True
    ).astype(jnp.bfloat16)


def local(slab, panels, pivots):
    rows_local, cols_local = slab.shape
    row_start = lax.axis_index("prow") * rows_local
    global_rows = row_start + jnp.arange(rows_local, dtype=jnp.int32)
    steps = jnp.arange(BLOCK_COLS, dtype=jnp.int32)
    whole_panels = lax.all_gather(panels, "pcol", axis=2, tiled=True)
    current = slab
    owner = 0 // rows_local
    panel_rows = panels[0]
    pivot_row = pivots[0]
    pointer, top_source = swap_sources(pivot_row, 0)
    local_source = top_source - row_start
    is_mine = (local_source >= 0) & (local_source < rows_local)
    fetched = jnp.take(current, jnp.clip(local_source, 0, rows_local - 1), axis=0)
    picked = jnp.where(is_mine[:, None], fetched.astype(jnp.float32), 0.0)
    old_top = picked_2(current, "prow", owner)
    diagonal_part = picked_2(panel_rows, "prow", owner)
    diagonal = lax.all_gather(diagonal_part, "pcol", axis=1, tiled=True).astype(jnp.float32)
    top_slice = sum_at_owner(picked.astype(jnp.bfloat16), "prow", 1)
    upper_slice = triangle(diagonal, top_slice)
    upper_rows = lax.all_gather(upper_slice, "prow", axis=1, tiled=True)
    match = global_rows[:, None] == pivot_row[None, :]
    last_hit = jnp.max(jnp.where(match, steps[None, :], -1), axis=1)
    displaced = (last_hit >= 0) & (global_rows >= BLOCK_COLS)
    moved = jnp.take(old_top, jnp.take(pointer, jnp.clip(last_hit, 0, BLOCK_COLS - 1)), axis=0)
    swapped = jnp.where(displaced[:, None], moved, current)
    product = jnp.dot(whole_panels[0], upper_rows, preferred_element_type=jnp.float32)
    updated = (swapped.astype(jnp.float32) - product).astype(jnp.bfloat16)
    upper_here = jnp.take(upper_rows, jnp.clip(global_rows - 0, 0, BLOCK_COLS - 1), axis=0)
    inside_top = (global_rows < BLOCK_COLS)[:, None]
    above_top = (global_rows < 0)[:, None]
    current = jnp.where(above_top, current, jnp.where(inside_top, upper_here, updated))
    return current


def solution(mesh):
    in_specs = (P("prow", "pcol"), P(None, "prow", "pcol"), P())
    out_specs = P("prow", "pcol")
    return jax.shard_map(local, mesh=mesh, in_specs=in_specs, out_specs=out_specs, check_vma=False)
```

profile of v0, /device:TPU:6, one launch (start us, length us, event | category | flops | bytes accessed | tf_op | source)
XLA Modules:
  0.0 302.3 jit_solution(2065237557100969711)
XLA Ops:
  8.0 1.5 select_reduce_fusion
  9.5 3.5 %gather_fusion = s32[512]{0:T(512)S(1)} fusion(s32[512]{0:T(512)S(1)} %get-tuple-element.60, s32[1024]{0:T(1024)S(1)} %pad_clamp_fusion.14), kind=kCustom, calls=%fused_computation.clone | custom fusion | bytes 6144 | tf_op jit(solution)/shard_map/jit(_take)/gather | solution.py:33
  13.0 3.5 %gather_fusion.1 = s32[512]{0:T(512)S(1)} fusion(s32[512]{0:T(512)S(1)} %get-tuple-element.55, s32[1024]{0:T(1024)S(1)} %pad_clamp_fusion.13), kind=kCustom, calls=%fused_computation.2.clone | custom fusion | bytes 6144 | tf_op jit(solution)/shard_map/jit(_take)/gather | solution.py:33
  16.6 3.5 %gather_fusion.2 = s32[512]{0:T(512)S(1)} fusion(s32[512]{0:T(512)S(1)} %get-tuple-element.53, s32[1024]{0:T(1024)S(1)} %pad_clamp_fusion.12), kind=kCustom, calls=%fused_computation.3.clone | custom fusion | bytes 6144 | tf_op jit(solution)/shard_map/jit(_take)/gather | solution.py:33
  20.1 3.5 %gather_fusion.3 = s32[512]{0:T(512)S(1)} fusion(s32[512]{0:T(512)S(1)} %get-tuple-element.51, s32[1024]{0:T(1024)S(1)} %pad_clamp_fusion.11), kind=kCustom, calls=%fused_computation.4.clone | custom fusion | bytes 6144 | tf_op jit(solution)/shard_map/jit(_take)/gather | solution.py:33
  23.6 3.5 %gather_fusion.4 = s32[512]{0:T(512)S(1)} fusion(s32[512]{0:T(512)S(1)} %get-tuple-element.49, s32[1024]{0:T(1024)S(1)} %pad_clamp_fusion.10), kind=kCustom, calls=%fused_computation.5.clone | custom fusion | bytes 6144 | tf_op jit(solution)/shard_map/jit(_take)/gather | solution.py:33
  27.2 3.5 %gather_fusion.5 = s32[512]{0:T(512)S(1)} fusion(s32[512]{0:T(512)S(1)} %get-tuple-element.47, s32[1024]{0:T(1024)S(1)} %pad_clamp_fusion.9), kind=kCustom, calls=%fused_computation.6.clone | custom fusion | bytes 6144 | tf_op jit(solution)/shard_map/jit(_take)/gather | solution.py:33
  30.7 3.5 %gather_fusion.6 = s32[512]{0:T(512)S(1)} fusion(s32[512]{0:T(512)S(1)} %get-tuple-element.45, s32[1024]{0:T(1024)S(1)} %pad_clamp_fusion.8), kind=kCustom, calls=%fused_computation.7.clone | custom fusion | bytes 6144 | tf_op jit(solution)/shard_map/jit(_take)/gather | solution.py:33
  34.2 3.5 %gather_fusion.7 = s32[512]{0:T(512)S(1)} fusion(s32[512]{0:T(512)S(1)} %get-tuple-element.43, s32[1024]{0:T(1024)S(1)} %pad_clamp_fusion.7), kind=kCustom, calls=%fused_computation.8.clone | custom fusion | bytes 6144 | tf_op jit(solution)/shard_map/jit(_take)/gather | solution.py:33
  37.8 3.5 %gather_fusion.8 = s32[512]{0:T(512)S(1)} fusion(s32[512]{0:T(512)S(1)} %get-tuple-element.41, s32[1024]{0:T(1024)S(1)} %pad_clamp_fusion.6), kind=kCustom, calls=%fused_computation.9.clone | custom fusion | bytes 6144 | tf_op jit(solution)/shard_map/jit(_take)/gather | solution.py:33
  41.3 3.5 %gather_fusion.9 = s32[512]{0:T(512)S(1)} fusion(s32[512]{0:T(512)S(1)} %get-tuple-element.39, s32[1024]{0:T(1024)S(1)} %pad_clamp_fusion.5), kind=kCustom, calls=%fused_computation.10.clone | custom fusion | bytes 6144 | tf_op jit(solution)/shard_map/jit(_take)/gather | solution.py:33
  44.8 3.5 %gather_fusion.10 = s32[512]{0:T(512)S(1)} fusion(s32[512]{0:T(512)S(1)} %and_select_fusion, s32[1024]{0:T(1024)S(1)} %pad_clamp_fusion.4), kind=kCustom, calls=%fused_computation.11.clone | custom fusion | bytes 6144 | tf_op jit(solution)/shard_map/jit(_take)/gather | solution.py:37
  48.4 2.0 gather_fusion.11
  50.6 0.8 copy.28
  51.4 16.5 %all-to-all-start = ((bf16[32,512,8]{1,2,0:T(8,128)(2,1)}), bf16[32,512,8]{1,2,0:T(8,128)(2,1)S(1)}, u32[]{:S(2)}, u32[]{:S(2)}) async-start(bf16[32,512,8]{1,2,0:T(8,128)(2,1)} %bitcast.4), calls=%async_computation | async-start | bytes 524288 | tf_op jit(solution)/shard_map/all_to_all | solution.py:20
  68.1 3.5 %gather_fusion.13 = s32[512]{0:T(512)S(1)} fusion(s32[512]{0:T(512)S(1)} %and_select_fusion, s32[1024]{0:T(1024)S(1)} %pad_clamp_fusion.1), kind=kCustom, calls=%fused_computation.12.clone | custom fusion | bytes 6144 | tf_op jit(solution)/shard_map/jit(_take)/gather | solution.py:72
  71.7 19.8 %all_gather.23 = bf16[1,512,512]{1,2,0:T(8,128)(2,1)S(1)} all-gather(bf16[1,512,32]{1,2,0:T(8,128)(2,1)S(1)} %copy-done.1), channel_id=1, replica_groups=mesh['prow'=32,'pcol'=16] {'pcol'}, dimensions={2}, use_global_device_ids=true | all-gather | bytes 557056 | tf_op jit(solution)/shard_map/all_gather | solution.py:53
  91.6 55.6 %all-gather.5.cloned.1.call-done = bf16[32,512,32]{1,2,0:T(8,128)(2,1)} async-done(((bf16[1,512,32]{1,2,0:T(8,128)(2,1)}), bf16[32,512,32]{1,2,0:T(8,128)(2,1)}) %all-gather.5.cloned.1.call-update) | async-done | bytes 1048592 | tf_op jit(solution)/shard_map/all_gather | solution.py:10
  147.2 0.8 dynamic_slice.10
  147.9 19.6 %all-gather = bf16[1,512,512]{1,2,0:T(8,128)(2,1)S(1)} all-gather(bf16[1,512,32]{1,2,0:T(8,128)(2,1)S(1)} %dynamic_slice.10), channel_id=2, replica_groups=mesh['prow'=32,'pcol'=16] {'pcol'}, dimensions={2}, use_global_device_ids=true | all-gather | bytes 557056 | tf_op jit(solution)/shard_map/all_gather | solution.py:65
  167.8 8.5 %while.1 = (s32[]{:T(128)}, f32[512,512]{0,1:T(8,128)S(1)}, s32[4,2]{0,1:T(2,128)S(1)}, f32[4,128,128]{2,1,0:T(8,128)S(1)}, s32[]{:T(128)}) while((s32[]{:T(128)}, f32[512,512]{0,1:T(8,128)S(1)}, s32[4,2]{0,1:T(2,128)S(1)}, f32[4,128,128]{2,1,0:T(8,128)S(1)}, s32[]{:T(128)}) %tuple.43), condition=%wide.while_cond, body=%wide.while_body.sunk | while | flops 2 | bytes 393329 | solution.py:43
  168.4 1.4 dynamic-slice.7
  170.5 1.4 dynamic-slice.7
  172.6 1.4 dynamic-slice.7
  174.7 1.4 dynamic-slice.7
  176.2 39.3 %custom-call.4 = f32[4,128,128]{1,2,0:T(8,128)S(1)} custom-call(f32[4,128,128]{2,1,0:T(8,128)S(1)} %get-tuple-element.14), custom_call_target="InvertDiagBlocksLowerTriangular" | custom-call | tf_op jit(solution)/shard_map/jit(_solve_triangular)/triangular_solve | solution.py:43
  216.9 63.4 %all_gather.20 = bf16[512,256]{0,1:T(8,128)(2,1)S(1)} all-gather(bf16[512,8]{0,1:T(8,128)(2,1)S(1)} %pad_maximum_fusion), channel_id=1, replica_groups=mesh['prow'=32,'pcol'=16] {'prow'}, dimensions={1}, use_global_device_ids=true | all-gather | bytes 270336 | tf_op jit(solution)/shard_map/all_gather | solution.py:68
  280.4 2.0 gather_fusion.12
  282.5 8.7 %all-gather.7.cloned.1.call-done = bf16[16384,256]{1,0:T(8,128)(2,1)} async-done(((bf16[512,256]{1,0:T(8,128)(2,1)}), bf16[16384,256]{1,0:T(8,128)(2,1)}) %all-gather.7.cloned.1.call-update) | async-done | bytes 8388624 | tf_op jit(solution)/shard_map/all_gather | solution.py:10
  291.2 1.0 slice.77
  292.2 2.0 gather_fusion.14
  294.6 0.8 copy.34
  (82 shorter events, 7.2 us)
Async XLA Ops:
  6.5 140.6 %all-gather.5.cloned.1.call-start = ((), (), s32[]{:S(2)}) async-start(), calls=%async_computation.1 | async-start | bytes 1081344 | tf_op jit(solution)/shard_map/all_gather | solution.py:10
  7.3 283.9 %all-gather.7.cloned.1.call-start = ((), (), s32[]{:S(2)}) async-start(), calls=%async_computation.2 | async-start | bytes 8650752 | tf_op jit(solution)/shard_map/all_gather | solution.py:10
  20.1 28.2 %copy-start.2 = (s32[1,512]{1,0:T(1,128)S(1)}, s32[1,512]{1,0:T(1,128)}, u32[]{:S(2)}) copy-start(s32[1,512]{1,0:T(1,128)} %param.9) | copy-start | bytes 6148
  20.1 28.3 %copy-start = (bf16[512,256]{1,0:T(8,128)(2,1)S(1)}, bf16[512,256]{1,0:T(8,128)(2,1)}, u32[]{:S(2)}) copy-start(bf16[512,256]{1,0:T(8,128)(2,1)} %param.7) | copy-start | bytes 786436
  30.7 41.0 %copy-start.1 = (bf16[1,512,32]{1,2,0:T(8,128)(2,1)S(1)}, bf16[1,512,32]{1,2,0:T(8,128)(2,1)}, u32[]{:S(2)}) copy-start(bf16[1,512,32]{1,2,0:T(8,128)(2,1)} %param.8) | copy-start | bytes 98308
  51.4 40.1 %all-to-all-start = ((bf16[32,512,8]{1,2,0:T(8,128)(2,1)}), bf16[32,512,8]{1,2,0:T(8,128)(2,1)S(1)}, u32[]{:S(2)}, u32[]{:S(2)}) async-start(bf16[32,512,8]{1,2,0:T(8,128)(2,1)} %bitcast.4), calls=%async_computation | async-start | bytes 524288 | tf_op jit(solution)/shard_map/all_to_all | solution.py:20
Sparse Core Ops, SparseCore 0:
  9.4 137.7 all-gather.4
  149.2 141.8 all-gather.6
where the time goes:
time: 303 us; the launch traced here: 302 us
  blocking collectives  103 us (34%)
  waiting for transfers between devices  65.7 us (22%)
  local copies, waits for them, and re-layouts  60.1 us (20%)
  other arithmetic  41.5 us (14%)
  starting transfers between devices  16.5 us (5%)
  between operations  13.9 us (5%)
    all_gather x2, waiting for transfers between devices, picked_2(): lax.all_gather(x, axis)  64.3 us
    all_gather x1, blocking collectives, local(): upper_rows = lax.all_gather(upper_slice, 'prow', axis=1, tiled=True)  63.4 us
    another operation x5, other arithmetic, triangle(): jax.scipy.linalg.solve_triangular(diagonal, right_side, lower=True, unit_...  39.5 us
    gather x10, local copies, waits for them, and re-layouts, swap_sources(): pointer = jnp.take(pointer, pointer)  34.9 us
    all_gather x1, blocking collectives, local(): whole_panels = lax.all_gather(panels, 'pcol', axis=2, tiled=True)  19.8 us
    all_gather x1, blocking collectives, local(): lax.all_gather(diagonal_part, 'pcol', axis=1, tiled=True)  19.6 us
    all_to_all x1, starting transfers between devices, sum_at_owner(): lax.all_to_all(pieces, axis, split_axis=0, concat_axis=0, tiled=True)  16.5 us
    another operation x20, local copies, waits for them, and re-layouts  8.33 us
  transfers between devices with their start and end apart: 3, of which 2 were waited for; matrix products, arithmetic and copies ran while one was open for 33% of the time, Pallas kernels for 0%

commit v1 on v0

v1 whole, which is shorter than its diff:
```python
import jax
import jax.numpy as jnp
from jax import lax
from jax.experimental import pallas as pl
from jax.experimental.pallas import tpu as pltpu
from jax.sharding import PartitionSpec as P

BLOCK = 512
CAP = 32
NZ = 16
MESH = pl.DeviceIdType.MESH
F32 = jnp.float32
BF16 = jnp.bfloat16
I32 = jnp.int32


def general(slab, panels, pivots):
    def gathered(x, axis):
        n = lax.axis_size(axis)
        return lax.all_to_all(jnp.broadcast_to(x[None], (n, *x.shape)), axis, 0, 0, tiled=True)

    rows_local, cols_local = slab.shape
    row_start = lax.axis_index("prow") * rows_local
    global_rows = row_start + jnp.arange(rows_local, dtype=I32)
    steps = jnp.arange(BLOCK, dtype=I32)
    pivot_row = pivots[0]
    earlier = steps[:, None] < steps[None, :]
    hit = (pivot_row[:, None] == steps[None, :]) & earlier
    parent = jnp.max(jnp.where(hit, steps[:, None], -1), axis=0)
    pointer = jnp.where(parent >= 0, parent, steps)
    pointer = lax.fori_loop(0, 10, lambda _, p: jnp.take(p, p), pointer)
    same = (pivot_row[:, None] == pivot_row[None, :]) & earlier
    latest = jnp.max(jnp.where(same, steps[:, None], -1), axis=0)
    top_source = jnp.where(latest >= 0, jnp.take(pointer, jnp.clip(latest, 0, BLOCK - 1)), pivot_row)
    local_source = top_source - row_start
    is_mine = (local_source >= 0) & (local_source < rows_local)
    fetched = jnp.take(slab, jnp.clip(local_source, 0, rows_local - 1), axis=0)
    picked = jnp.where(is_mine[:, None], fetched, jnp.zeros_like(fetched))
    top = gathered(picked, "prow").astype(F32).sum(axis=0)
    old_top = gathered(slab, "prow")[0]
    diagonal = gathered(gathered(panels[0], "prow")[0], "pcol")
    diagonal = jnp.moveaxis(diagonal, 0, 1).reshape(BLOCK, BLOCK).astype(F32)
    upper = jax.scipy.linalg.solve_triangular(diagonal, top, lower=True, unit_diagonal=True).astype(BF16)
    match = global_rows[:, None] == pivot_row[None, :]
    last_hit = jnp.max(jnp.where(match, steps[None, :], -1), axis=1)
    displaced = (last_hit >= 0) & (global_rows >= BLOCK)
    moved = jnp.take(old_top, jnp.take(pointer, jnp.clip(last_hit, 0, BLOCK - 1)), axis=0)
    swapped = jnp.where(displaced[:, None], moved, slab)
    whole = jnp.moveaxis(gathered(panels[0], "pcol"), 0, 1).reshape(rows_local, BLOCK)
    product = jnp.dot(whole, upper, preferred_element_type=F32)
    updated = (swapped.astype(F32) - product).astype(BF16)
    return jnp.where(row_start == 0, upper, updated)


def iota(shape, dim):
    return lax.broadcasted_iota(I32, shape, dim)


def ones(mask):
    return jnp.where(mask, 1.0, 0.0).astype(BF16)


def dot(a, b):
    return jnp.dot(a, b, preferred_element_type=F32)


def dot_nt(a, b):
    return lax.dot_general(a, b, (((1,), (1,)), ((), ())), preferred_element_type=F32)


def dot_f32(a, b):
    return jnp.dot(a, b, preferred_element_type=F32, precision=lax.Precision.HIGHEST)


def column(row):
    n = row.shape[1]
    blocks = [jnp.broadcast_to(row[:, i : i + 128], (128, 128)).astype(F32).T[:, :1] for i in range(0, n, 128)]
    return jnp.concatenate(blocks, axis=0).astype(I32)


def lower_inverse(block):
    i, j = iota((128, 128), 0), iota((128, 128), 1)
    eye = jnp.where(i == j, 1.0, 0.0)
    inv = []
    for d in range(4):
        full = block(d, d)
        n = jnp.where((i // 16 == j // 16) & (i > j), full, 0.0)
        m, p = eye - n, n
        for _ in range(3):
            p = dot_f32(p, p)
            m = m + dot_f32(m, p)
        for size in (16, 32, 64):
            b = jnp.where((i // (2 * size) == j // (2 * size)) & (i // size > j // size), full, 0.0)
            m = m - dot_f32(m, dot_f32(b, m))
        inv.append(m)
    lower = {}
    for d in (0, 2):
        lower[d] = -dot_f32(inv[d + 1], dot_f32(block(d + 1, d), inv[d]))
    zero = jnp.zeros((128, 128), F32)
    first = jnp.concatenate([jnp.concatenate([inv[0], zero], 1), jnp.concatenate([lower[0], inv[1]], 1)], 0)
    second = jnp.concatenate([jnp.concatenate([inv[2], zero], 1), jnp.concatenate([lower[2], inv[3]], 1)], 0)
    corner = jnp.concatenate(
        [jnp.concatenate([block(2, 0), block(2, 1)], 1), jnp.concatenate([block(3, 0), block(3, 1)], 1)], 0
    )
    third = -dot_f32(second, dot_f32(corner, first))
    zero = jnp.zeros((256, 256), F32)
    return jnp.concatenate([jnp.concatenate([first, zero], 1), jnp.concatenate([third, second], 1)], 0)


def kernel(
    slab, panel, pivot, out, over,
    cand, pbuf, lbuf, zbuf, zsend,
    c_send, c_recv, p_send, p_recv, l_send, l_recv, lz_send, z_send, z_recv, ready,
):
    r, c = lax.axis_index("prow"), lax.axis_index("pcol")
    y, z = r // NZ, r % NZ

    def at(dz):
        return (y * NZ + (z + dz + NZ) % NZ, c)

    partner = ((1 - y) * NZ + z, c)
    root = (0, c)

    def peer(i):
        return (r, (c + i) % 16)

    def copy(src, dst, send, recv, device):
        return pltpu.make_async_remote_copy(
            src_ref=src, dst_ref=dst, send_sem=send, recv_sem=recv, device_id=device, device_id_type=MESH
        )

    near = (1, -1, 2, -2, 3, -3, 4, -4)
    barrier = pltpu.get_barrier_semaphore()

    def hello(device):
        pl.semaphore_signal(barrier, inc=1, device_id=device, device_id_type=MESH)

    for dz in near:
        hello(at(dz))
    hello(partner)
    for i in range(1, 16):
        hello(peer(i))
    far_from_root = (y == 0) & (z > 4) & (z < 12)

    @pl.when(r == 0)
    def _():
        for dz in range(5, 12):
            hello((dz, c))

    p_row = pivot[...]
    b_row = p_row // BLOCK
    k_row = iota((1, BLOCK), 1)
    before = iota((BLOCK, BLOCK), 0) < iota((BLOCK, BLOCK), 1)
    in_block = iota((32, BLOCK), 0) == b_row
    counts = dot(ones(in_block), ones(before))
    rank_row = jnp.sum(jnp.where(in_block, counts, 0.0), axis=0, keepdims=True).astype(I32)
    p_col = column(p_row)
    equal = p_col == p_row
    later_row = jnp.max(jnp.where(equal & (iota((BLOCK, BLOCK), 0) > iota((BLOCK, BLOCK), 1)), 1, 0), axis=0, keepdims=True)
    hit_row = jnp.max(jnp.where(p_col == iota((BLOCK, BLOCK), 1), 1, 0), axis=0, keepdims=True)
    goes_on = ones((p_row < BLOCK) | (later_row > 0))
    next_goes_on = dot(goes_on, ones(iota((BLOCK, BLOCK), 0) == p_row))
    stays_row = ones((hit_row > 0) | (later_row > 0) | (next_goes_on > 0))
    rank0_row = dot(stays_row, ones(before)).astype(I32)
    far_row = p_row >= BLOCK
    slots = iota((CAP, BLOCK), 0)
    mine = jnp.where((b_row == r) & far_row, 1, 0) * jnp.where(rank_row == slots, 1, 0)
    local_hit = ones(iota((BLOCK, BLOCK), 0) + r * BLOCK == p_row)
    pack = dot_nt(ones(mine > 0), local_hit)
    pack0 = jnp.where((rank0_row == slots) & (stays_row > 0), 1.0, 0.0)
    pack = jnp.where(r == 0, pack0, pack).astype(BF16)
    cand[r] = dot(pack, slab[...]).astype(BF16)
    full = jnp.max(jnp.where(far_row, rank_row, 0), axis=1, keepdims=True)
    full0 = jnp.max(jnp.where(stays_row > 0, rank0_row, 0), axis=1, keepdims=True)
    over[0, 0] = jnp.max(jnp.maximum(full, full0))
    pbuf[c] = panel[...]

    pl.semaphore_wait(barrier, 24 + jnp.where(far_from_root, 1, 0))

    sends, c_wait = [], {}

    def send_cand(n, slot, device):
        t = copy(cand.at[slot], cand.at[slot], c_send.at[n], c_recv.at[slot], device)
        t.start()
        sends.append(t)

    def wait_cand(slot):
        copy(cand.at[slot], cand.at[slot], c_send.at[0], c_recv.at[slot], partner).wait_recv()

    def slot_of(dz):
        return y * NZ + (z + dz + NZ) % NZ

    for n, dz in enumerate((4, -4, 3, -3, 2, -2, 1, -1)):
        send_cand(n, r, at(dz))
    send_cand(8, r, partner)

    @pl.when((y == 0) & (z > 0))
    def _():
        pl.semaphore_signal(ready.at[z], inc=1, device_id=root, device_id_type=MESH)

    for i in range(1, 16):
        copy(panel, pbuf.at[c], p_send.at[i], p_recv.at[c], peer(i)).start()

    @pl.when(r == 0)
    def _():
        for dz in (1, 2, 3, 4, 15, 14, 13, 12, 5, 6, 7, 11, 10, 9, 8):
            pl.semaphore_wait(ready.at[dz], 1)
            copy(panel, lbuf.at[c], lz_send.at[dz], l_recv.at[c], (dz, c)).start()
        copy(panel, lbuf.at[c], lz_send.at[0], l_recv.at[c], partner).start()

    kk = iota((BLOCK, BLOCK), 0)
    jj = iota((BLOCK, BLOCK), 1)
    parent = jnp.max(jnp.where((p_row == kk) & (jj < kk), jj, -1), axis=1, keepdims=True)
    k_col = iota((BLOCK, 1), 0)
    chain = ones(jnp.where(parent >= 0, parent, k_col) == jj)

    def square(times, a):
        for _ in range(times):
            a = dot(a, a).astype(BF16)
        return a

    chain = square(4, chain)

    n = 9
    for dz in (4, 3, 2, 1):
        wait_cand(slot_of(dz))
        send_cand(n, slot_of(dz), at(-4))
        n += 1
        wait_cand(slot_of(-dz))
        if dz < 4:
            send_cand(n, slot_of(-dz), at(4))
            n += 1
    for dz in (4, -4, 3, -3, 2, -2, 1, -1):
        send_cand(n, slot_of(dz), partner)
        n += 1

    chain = square(5, chain)
    slot_row = jnp.where(far_row, b_row * CAP + rank_row, -1)

    @pl.when(r == 0)
    def _():
        content = dot(chain, slab[...]).astype(BF16)
        for q in range(0, 32, 4):
            pick = ones(slot_row == iota((4 * CAP, BLOCK), 0) + q * CAP)
            zsend[q : q + 4] = dot(pick, content).astype(BF16).reshape(4, CAP, 256)

    latest = jnp.max(jnp.where(equal & (jj < kk), jj, -1), axis=1, keepdims=True)
    source = dot(ones(latest == jj), chain) + jnp.where((latest < 0) & (p_col == jj), 1.0, 0.0)
    rank0_col = column(jnp.where(stays_row > 0, rank0_row, -1))
    near_pick = dot(source.astype(BF16), ones(rank0_col == iota((BLOCK, CAP), 1)))
    slot_col = column(slot_row)
    far_pick = ones((slot_col == iota((BLOCK, 32 * CAP), 1)) & (latest < 0))
    pick = jnp.concatenate([near_pick.astype(BF16), far_pick[:, CAP:]], axis=1)

    for dz in (5, 6, 7, 8, -5, -6, -7):
        wait_cand(slot_of(dz))
        send_cand(n, slot_of(dz), partner)
        n += 1

    @pl.when(r == 0)
    def _():
        for dz in range(1, NZ):
            copy(zsend.at[dz], zbuf.at[0], z_send.at[dz], z_recv.at[0], (dz, c)).start()
            copy(zsend.at[NZ + dz], zbuf.at[1], z_send.at[NZ + dz], z_recv.at[1], (dz, c)).start()
        copy(zsend.at[NZ], zbuf.at[0], z_send.at[NZ], z_recv.at[0], partner).start()

    def wait_shard(buf, sem, i):
        copy(buf.at[i], buf.at[i], p_send.at[1], sem.at[i], partner).wait_recv()

    @pl.when(r > 0)
    def _():
        wait_shard(lbuf, l_recv, c)

        @pl.when(y == 0)
        def _():
            copy(lbuf.at[c], lbuf.at[c], l_send.at[0], l_recv.at[c], partner).start()

        for i in range(1, 16):
            copy(lbuf.at[c], lbuf.at[c], l_send.at[i], l_recv.at[c], peer(i)).start()

    for i in range(1, 16):
        wait_shard(pbuf, p_recv, (c + i) % 16)

    @pl.when(r == 0)
    def _():
        lbuf[...] = pbuf[...]

    @pl.when(r > 0)
    def _():
        for i in range(1, 16):
            wait_shard(lbuf, l_recv, (c + i) % 16)

    panel_t = pbuf[...].reshape(BLOCK, BLOCK)
    diagonal_t = lbuf[...].reshape(BLOCK, BLOCK)

    def block(a, b):
        return diagonal_t[128 * b : 128 * b + 128, 128 * a : 128 * a + 128].astype(F32).T

    inverse = lower_inverse(block)
    high = inverse.astype(BF16)
    low = (inverse - high.astype(F32)).astype(BF16)

    for dz in range(NZ):
        wait_cand((1 - y) * NZ + dz)
    top = dot(pick, cand[...].reshape(32 * CAP, 256)).astype(BF16)
    upper = (dot(high, top) + dot(low, top)).astype(BF16)

    @pl.when(r > 0)
    def _():
        copy(zbuf.at[0], zbuf.at[0], z_send.at[0], z_recv.at[0], partner).wait_recv()

        @pl.when((y == 0) & (z > 0))
        def _():
            copy(zbuf.at[1], zbuf.at[1], z_send.at[0], z_recv.at[1], partner).wait_recv()
            copy(zbuf.at[1], zbuf.at[0], z_send.at[0], z_recv.at[0], partner).start()

        last = jnp.where(later_row > 0, 0, mine)
        place = dot_nt(local_hit, ones(last > 0))
        moved = dot(place.astype(BF16), zbuf[0])
        hit = jnp.sum(place, axis=1, keepdims=True) > 0
        product = lax.dot_general(panel_t, upper, (((0,), (0,)), ((), ())), preferred_element_type=F32)
        out[...] = (jnp.where(hit, moved, slab[...].astype(F32)) - product).astype(BF16)

    @pl.when(r == 0)
    def _():
        out[...] = upper

    for t in sends:
        t.wait_send()
    for i in range(1, 16):
        copy(panel, pbuf.at[c], p_send.at[i], p_recv.at[c], peer(i)).wait_send()

    @pl.when(r > 0)
    def _():
        for i in range(1, 16):
            copy(lbuf.at[c], lbuf.at[c], l_send.at[i], l_recv.at[c], peer(i)).wait_send()

        @pl.when(y == 0)
        def _():
            copy(lbuf.at[c], lbuf.at[c], l_send.at[0], l_recv.at[c], partner).wait_send()
            copy(zbuf.at[1], zbuf.at[0], z_send.at[0], z_recv.at[0], partner).wait_send()

    @pl.when(r == 0)
    def _():
        for dz in range(NZ):
            copy(panel, lbuf.at[c], lz_send.at[dz], l_recv.at[c], partner).wait_send()
        for dz in range(1, 32):
            copy(zsend.at[dz], zbuf.at[0], z_send.at[dz], z_recv.at[0], partner).wait_send()


def local(slab, panels, pivots):
    vmem = pl.BlockSpec(memory_space=pltpu.VMEM)
    dma = pltpu.SemaphoreType.DMA
    out, over = pl.pallas_call(
        kernel,
        out_shape=(jax.ShapeDtypeStruct(slab.shape, BF16), jax.ShapeDtypeStruct((1, 1), I32)),
        in_specs=[vmem] * 3,
        out_specs=(vmem, pl.BlockSpec(memory_space=pltpu.SMEM)),
        scratch_shapes=[
            pltpu.VMEM((32, CAP, 256), BF16),
            pltpu.VMEM((16, 32, BLOCK), BF16),
            pltpu.VMEM((16, 32, BLOCK), BF16),
            pltpu.VMEM((2, CAP, 256), BF16),
            pltpu.VMEM((32, CAP, 256), BF16),
            dma((32,)), dma((32,)), dma((16,)), dma((16,)), dma((16,)), dma((16,)), dma((16,)), dma((32,)), dma((2,)),
            pltpu.SemaphoreType.REGULAR((16,)),
        ],
        compiler_params=pltpu.CompilerParams(collective_id=0, has_side_effects=True),
        name="lu_update",
    )(slab, jnp.transpose(panels[0]), pivots)
    return lax.cond(over[0, 0] >= CAP, general, lambda *_: out, slab, panels, pivots)


def solution(mesh):
    in_specs = (P("prow", "pcol"), P(None, "prow", "pcol"), P())
    out_specs = P("prow", "pcol")
    return jax.shard_map(local, mesh=mesh, in_specs=in_specs, out_specs=out_specs, check_vma=False)
```

time: 303 us -> 55.8 us (0.18)
  the two profiles are of different devices: /device:TPU:6 before, /device:TPU:93 now
where the time goes in v1:
time: 55.8 us; the launch traced here: 55.7 us
  Pallas kernels  54.3 us (97%)
  local copies, waits for them, and re-layouts  0.71 us (1%)
  between operations  0.65 us (1%)
    pallas_call x1, Pallas kernels, local(): pl.pallas_call(kernel, out_shape=(jax.ShapeDtypeStruct(slab.shape, BF16),...  54.3 us

profile of v1, /device:TPU:93, one launch (start us, length us, event | category | flops | bytes accessed | tf_op | source)
XLA Modules:
  0.0 55.7 jit_solution(14052870291400254094)
XLA Ops:
  0.0 54.3 %lu_update.1 = (bf16[512,256]{1,0:T(8,128)(2,1)S(1)}, s32[1,1]{1,0:T(1,128)}) custom-call(bf16[512,256]{1,0:T(8,128)(2,1)} %slab.1, bf16[32,512]{1,0:T(8,128)(2,1)} %bitcast.61, s32[1,512]{1,0:T(1,128)} %pivot.1), custom_call_target="tpu_custom_call" | custom-call | tf_op jit(solution)/shard_map/lu_update/pallas_call | solution.py:354
  55.0 0.7 %copy.33 = bf16[512,256]{1,0:T(8,128)(2,1)} copy(bf16[512,256]{1,0:T(8,128)(2,1)S(1)} %get-tuple-element.36) | data formatting | bytes 524288
  (1 shorter events, 0.0 us)

commit v2 on v1

v2 whole, which is shorter than its diff:
```python
import jax
import jax.numpy as jnp
from jax import lax
from jax.experimental import pallas as pl
from jax.experimental.pallas import tpu as pltpu
from jax.sharding import PartitionSpec as P

BLOCK = 512
CAP = 32
NZ = 16
MESH = pl.DeviceIdType.MESH
F32 = jnp.float32
BF16 = jnp.bfloat16
I32 = jnp.int32


def general(slab, panels, pivots):
    def gathered(x, axis):
        n = lax.axis_size(axis)
        return lax.all_to_all(jnp.broadcast_to(x[None], (n, *x.shape)), axis, 0, 0, tiled=True)

    rows_local, cols_local = slab.shape
    row_start = lax.axis_index("prow") * rows_local
    global_rows = row_start + jnp.arange(rows_local, dtype=I32)
    steps = jnp.arange(BLOCK, dtype=I32)
    pivot_row = pivots[0]
    earlier = steps[:, None] < steps[None, :]
    hit = (pivot_row[:, None] == steps[None, :]) & earlier
    parent = jnp.max(jnp.where(hit, steps[:, None], -1), axis=0)
    pointer = jnp.where(parent >= 0, parent, steps)
    pointer = lax.fori_loop(0, 10, lambda _, p: jnp.take(p, p), pointer)
    same = (pivot_row[:, None] == pivot_row[None, :]) & earlier
    latest = jnp.max(jnp.where(same, steps[:, None], -1), axis=0)
    top_source = jnp.where(latest >= 0, jnp.take(pointer, jnp.clip(latest, 0, BLOCK - 1)), pivot_row)
    local_source = top_source - row_start
    is_mine = (local_source >= 0) & (local_source < rows_local)
    fetched = jnp.take(slab, jnp.clip(local_source, 0, rows_local - 1), axis=0)
    picked = jnp.where(is_mine[:, None], fetched, jnp.zeros_like(fetched))
    top = gathered(picked, "prow").astype(F32).sum(axis=0)
    old_top = gathered(slab, "prow")[0]
    diagonal = gathered(gathered(panels[0], "prow")[0], "pcol")
    diagonal = jnp.moveaxis(diagonal, 0, 1).reshape(BLOCK, BLOCK).astype(F32)
    upper = jax.scipy.linalg.solve_triangular(diagonal, top, lower=True, unit_diagonal=True).astype(BF16)
    match = global_rows[:, None] == pivot_row[None, :]
    last_hit = jnp.max(jnp.where(match, steps[None, :], -1), axis=1)
    displaced = (last_hit >= 0) & (global_rows >= BLOCK)
    moved = jnp.take(old_top, jnp.take(pointer, jnp.clip(last_hit, 0, BLOCK - 1)), axis=0)
    swapped = jnp.where(displaced[:, None], moved, slab)
    whole = jnp.moveaxis(gathered(panels[0], "pcol"), 0, 1).reshape(rows_local, BLOCK)
    product = jnp.dot(whole, upper, preferred_element_type=F32)
    updated = (swapped.astype(F32) - product).astype(BF16)
    return jnp.where(row_start == 0, upper, updated)


def iota(shape, dim):
    return lax.broadcasted_iota(I32, shape, dim)


def ones(mask):
    return jnp.where(mask, 1.0, 0.0).astype(BF16)


def dot(a, b):
    return jnp.dot(a, b, preferred_element_type=F32)


def dot_nt(a, b):
    return lax.dot_general(a, b, (((1,), (1,)), ((), ())), preferred_element_type=F32)


def column(row):
    n = row.shape[1]
    blocks = [jnp.broadcast_to(row[:, i : i + 128], (128, 128)).astype(F32).T[:, :1] for i in range(0, n, 128)]
    return jnp.concatenate(blocks, axis=0).astype(I32)


def split(x):
    high = x.astype(BF16)
    return high, (x - high.astype(F32)).astype(BF16)


def dot_f32(a, b):
    a_parts = (a,) if a.dtype == BF16 else split(a)
    b_parts = (b,) if b.dtype == BF16 else split(b)
    total = dot(a_parts[0], b_parts[0])
    if len(b_parts) > 1:
        total += dot(a_parts[0], b_parts[1])
    if len(a_parts) > 1:
        total += dot(a_parts[1], b_parts[0])
    return total


def lower_inverse(block):
    i, j = iota((128, 128), 0), iota((128, 128), 1)
    eye = jnp.where(i == j, 1.0, 0.0)
    inv, full, power = [], [], []
    for d in range(4):
        full.append(block(d, d))
        n = jnp.where((i // 16 == j // 16) & (i > j), full[d].astype(F32), 0.0)
        inv.append(eye - n)
        power.append(n.astype(BF16))
    for _ in range(3):
        for d in range(4):
            power[d] = dot_f32(power[d], power[d])
        for d in range(4):
            inv[d] = inv[d] + dot_f32(inv[d], power[d])
    for size in (16, 32, 64):
        off = (i // (2 * size) == j // (2 * size)) & (i // size > j // size)
        step = [dot_f32(jnp.where(off, full[d].astype(F32), 0.0).astype(BF16), inv[d]) for d in range(4)]
        for d in range(4):
            inv[d] = inv[d] - dot_f32(inv[d], step[d])
    zero = jnp.zeros((128, 128), F32)
    halves = []
    for d in (0, 2):
        lower = -dot_f32(inv[d + 1], dot_f32(block(d + 1, d), inv[d]))
        halves.append(jnp.concatenate([jnp.concatenate([inv[d], zero], 1), jnp.concatenate([lower, inv[d + 1]], 1)], 0))
    return halves


def kernel(
    slab, panel, pivot, out, over,
    cand, pbuf, lbuf, zbuf, zsend, straight,
    c_send, c_recv, p_send, p_recv, l_send, l_recv, lz_send, z_send, z_recv, ready,
):
    r, c = lax.axis_index("prow"), lax.axis_index("pcol")
    y, z = r // NZ, r % NZ

    def ring(dz):
        return (z + dz + NZ) % NZ

    def at(dz):
        return (y * NZ + ring(dz), c)

    partner = ((1 - y) * NZ + z, c)

    def peer(i):
        return (r, (c + i) % 16)

    def copy(src, dst, send, recv, device):
        return pltpu.make_async_remote_copy(
            src_ref=src, dst_ref=dst, send_sem=send, recv_sem=recv, device_id=device, device_id_type=MESH
        )

    near = (4, -4, 3, -3, 2, -2, 1, -1)
    barrier = pltpu.get_barrier_semaphore()

    def hello(device):
        pl.semaphore_signal(barrier, inc=1, device_id=device, device_id_type=MESH)

    hello(partner)
    for i in range(1, 16):
        hello(peer(i))
    for dz in near:

        @pl.when(ring(dz) > z)
        def _(dz=dz):
            hello(at(dz))

    @pl.when(z == 0)
    def _():
        for dz in range(5, 12):
            hello(at(dz))

    p_row = pivot[...]
    b_row = p_row // BLOCK
    before = iota((BLOCK, BLOCK), 0) < iota((BLOCK, BLOCK), 1)
    in_block = iota((32, BLOCK), 0) == b_row
    counts = dot(ones(in_block), ones(before))
    rank_row = jnp.sum(jnp.where(in_block, counts, 0.0), axis=0, keepdims=True).astype(I32)
    p_col = column(p_row)
    equal = p_col == p_row
    later_row = jnp.max(jnp.where(equal & (iota((BLOCK, BLOCK), 0) > iota((BLOCK, BLOCK), 1)), 1, 0), axis=0, keepdims=True)
    hit_row = jnp.max(jnp.where(p_col == iota((BLOCK, BLOCK), 1), 1, 0), axis=0, keepdims=True)
    goes_on = ones((p_row < BLOCK) | (later_row > 0))
    next_goes_on = dot(goes_on, ones(iota((BLOCK, BLOCK), 0) == p_row))
    stays_row = ones((hit_row > 0) | (later_row > 0) | (next_goes_on > 0))
    rank0_row = dot(stays_row, ones(before)).astype(I32)
    far_row = p_row >= BLOCK
    slots = iota((CAP, BLOCK), 0)
    mine = jnp.where((b_row == r) & far_row, 1, 0) * jnp.where(rank_row == slots, 1, 0)
    local_hit = ones(iota((BLOCK, BLOCK), 0) + r * BLOCK == p_row)
    pack = dot_nt(ones(mine > 0), local_hit)
    pack0 = jnp.where((rank0_row == slots) & (stays_row > 0), 1.0, 0.0)
    pack = jnp.where(r == 0, pack0, pack).astype(BF16)
    cand[r] = dot(pack, slab[...]).astype(BF16)
    pbuf[c] = panel[...]

    @pl.when(r == 0)
    def _():
        lbuf[c] = panel[...]

    pl.semaphore_wait(
        barrier, 16 + jnp.minimum(z, 4) + jnp.maximum(z - 11, 0) + jnp.where((z > 4) & (z < 12), 1, 0)
    )

    def announce(device):
        pl.semaphore_signal(ready.at[z], inc=1, device_id=device, device_id_type=MESH)

    @pl.when((z > 4) & (z < 12))
    def _():
        announce((y * NZ, c))

    for dz in near:

        @pl.when(ring(dz) < z)
        def _(dz=dz):
            announce(at(dz))

    def send_cand(n, slot, device):
        t = copy(cand.at[slot], cand.at[slot], c_send.at[n], c_recv.at[slot], device)
        t.start()

    def wait_cand(slot):
        copy(cand.at[slot], cand.at[slot], c_send.at[0], c_recv.at[slot], partner).wait_recv()

    def slot_of(dz):
        return y * NZ + ring(dz)

    def send_shard(n, device):
        copy(lbuf.at[c], lbuf.at[c], lz_send.at[n], l_recv.at[c], device).start()

    def wait_shard(buf, sem, i):
        copy(buf.at[i], buf.at[i], p_send.at[1], sem.at[i], partner).wait_recv()

    @pl.when(r == 0)
    def _():
        send_shard(0, partner)

    for n, dz in enumerate(near):

        @pl.when(ring(dz) < z)
        def _(n=n, dz=dz):
            send_cand(n, r, at(dz))

    send_cand(8, r, partner)
    for i in range(1, 16):
        copy(panel, pbuf.at[c], p_send.at[i], p_recv.at[c], peer(i)).start()

    def spread_shard():
        for i in range(1, 16):
            copy(lbuf.at[c], lbuf.at[c], l_send.at[i], l_recv.at[c], peer(i)).start()

    @pl.when((r > 0) & (z < 5))
    def _():
        wait_shard(lbuf, l_recv, c)
        spread_shard()

    def root_sends(steps):
        @pl.when(z == 0)
        def _():
            for dz in steps:
                pl.semaphore_wait(ready.at[dz], 1)
                send_shard(dz, at(dz))
                if dz < 5 or dz > 11:
                    send_cand(near.index(dz if dz < 5 else dz - NZ), r, at(dz))

    root_sends((1, 2, 3, 4))

    kk = iota((BLOCK, BLOCK), 0)
    jj = iota((BLOCK, BLOCK), 1)
    parent = jnp.max(jnp.where((p_row == kk) & (jj < kk), jj, -1), axis=1, keepdims=True)
    k_col = iota((BLOCK, 1), 0)
    chain = ones(jnp.where(parent >= 0, parent, k_col) == jj)

    def square(times, a):
        for _ in range(times):
            a = dot(a, a).astype(BF16)
        return a

    for n, dz in enumerate(near):

        @pl.when((z > 0) & (ring(dz) > z))
        def _(n=n, dz=dz):
            pl.semaphore_wait(ready.at[ring(dz)], 1)
            send_cand(n, r, at(dz))

    chain = square(4, chain)
    root_sends((5, 15, 14, 13, 12, 6, 7, 11, 10, 9, 8))

    n = 9
    for dz in (4, 3, 2, 1):
        wait_cand(slot_of(dz))
        send_cand(n, slot_of(dz), at(-4))
        n += 1
        wait_cand(slot_of(-dz))
        if dz < 4:
            send_cand(n, slot_of(-dz), at(4))
            n += 1
    for dz in near:
        send_cand(n, slot_of(dz), partner)
        n += 1

    @pl.when(z > 4)
    def _():
        wait_shard(lbuf, l_recv, c)
        spread_shard()

    chain = square(5, chain)
    slot_row = jnp.where(far_row, b_row * CAP + rank_row, -1)

    @pl.when(r == 0)
    def _():
        content = dot(chain, slab[...]).astype(BF16)
        for q in range(0, 32, 4):
            pick = ones(slot_row == iota((4 * CAP, BLOCK), 0) + q * CAP)
            zsend[q : q + 4] = dot(pick, content).astype(BF16).reshape(4, CAP, 256)

    full = jnp.max(jnp.where(far_row, rank_row, 0), axis=1, keepdims=True)
    full0 = jnp.max(jnp.where(stays_row > 0, rank0_row, 0), axis=1, keepdims=True)
    over[0, 0] = jnp.max(jnp.maximum(full, full0))
    latest = jnp.max(jnp.where(equal & (jj < kk), jj, -1), axis=1, keepdims=True)
    source = dot(ones(latest == jj), chain) + jnp.where((latest < 0) & (p_col == jj), 1.0, 0.0)
    rank0_col = column(jnp.where(stays_row > 0, rank0_row, -1))
    near_pick = dot(source.astype(BF16), ones(rank0_col == iota((BLOCK, CAP), 1)))
    slot_col = column(slot_row)
    far_pick = ones((slot_col == iota((BLOCK, 32 * CAP), 1)) & (latest < 0))
    pick = jnp.concatenate([near_pick.astype(BF16), far_pick[:, CAP:]], axis=1)

    def other_ring():
        half = zsend.at[pl.ds(NZ, NZ)]
        return copy(half, half, z_send.at[0], z_recv.at[1], partner)

    @pl.when(r == 0)
    def _():
        other_ring().start()

    @pl.when(r == NZ)
    def _():
        other_ring().wait_recv()
        zbuf[...] = zsend[NZ]

    @pl.when(z == 0)
    def _():
        for dz in range(1, NZ):
            copy(zsend.at[y * NZ + dz], zbuf, z_send.at[dz], z_recv.at[0], at(dz)).start()

    for dz in (5, 6, 7, 8, -5, -6, -7):
        wait_cand(slot_of(dz))
        send_cand(n, slot_of(dz), partner)
        n += 1

    for i in range(1, 16):
        wait_shard(pbuf, p_recv, (c + i) % 16)

    @pl.when(r == 0)
    def _():
        for i in range(1, 16):
            lbuf[(c + i) % 16] = pbuf[(c + i) % 16]

    panel_t = pbuf[...].reshape(BLOCK, BLOCK)
    for a in range(0, BLOCK, 128):
        for b in range(0, BLOCK, 128):
            straight[b : b + 128, a : a + 128] = panel_t[a : a + 128, b : b + 128].astype(F32).T.astype(BF16)

    @pl.when(r > 0)
    def _():
        for i in range(1, 16):
            wait_shard(lbuf, l_recv, (c + i) % 16)

    diagonal_t = lbuf[...].reshape(BLOCK, BLOCK)

    def block(a, b):
        return diagonal_t[128 * b : 128 * b + 128, 128 * a : 128 * a + 128].astype(F32).T.astype(BF16)

    first, second = lower_inverse(block)
    corner = jnp.concatenate(
        [jnp.concatenate([block(2, 0), block(2, 1)], 1), jnp.concatenate([block(3, 0), block(3, 1)], 1)], 0
    )
    first_high, first_low = split(first)
    second_high, second_low = split(second)

    for dz in range(NZ):
        wait_cand((1 - y) * NZ + dz)
    top = dot(pick, cand[...].reshape(32 * CAP, 256))
    half = top[:256].astype(BF16)
    upper1 = dot(first_high, half) + dot(first_low, half)
    high1, low1 = split(upper1)
    high2, low2 = split(top[256:] - (dot(corner, high1) + dot(corner, low1)))
    upper2 = dot(second_high, high2) + dot(second_high, low2) + dot(second_low, high2)
    upper = jnp.concatenate([high1, upper2.astype(BF16)], axis=0)

    @pl.when(r > 0)
    def _():
        @pl.when(z > 0)
        def _():
            copy(zbuf, zbuf, z_send.at[0], z_recv.at[0], partner).wait_recv()

        last = jnp.where(later_row > 0, 0, mine)
        place = dot_nt(local_hit, ones(last > 0))
        moved = dot(place.astype(BF16), zbuf[...])
        hit = jnp.sum(place, axis=1, keepdims=True) > 0
        product = dot(straight[...], upper)
        out[...] = (jnp.where(hit, moved, slab[...].astype(F32)) - product).astype(BF16)

    @pl.when(r == 0)
    def _():
        out[...] = upper

    for i in range(31):
        copy(cand.at[r], cand.at[r], c_send.at[i], c_recv.at[r], partner).wait_send()
    for i in range(1, 16):
        copy(panel, pbuf.at[c], p_send.at[i], p_recv.at[c], peer(i)).wait_send()

    @pl.when(r > 0)
    def _():
        for i in range(1, 16):
            copy(lbuf.at[c], lbuf.at[c], l_send.at[i], l_recv.at[c], peer(i)).wait_send()

    @pl.when(z == 0)
    def _():
        for dz in range(1, NZ):
            copy(lbuf.at[c], lbuf.at[c], lz_send.at[dz], l_recv.at[c], partner).wait_send()
            copy(zsend.at[dz], zbuf, z_send.at[dz], z_recv.at[0], partner).wait_send()

    @pl.when(r == 0)
    def _():
        copy(lbuf.at[c], lbuf.at[c], lz_send.at[0], l_recv.at[c], partner).wait_send()
        other_ring().wait_send()


def local(slab, panels, pivots):
    vmem = pl.BlockSpec(memory_space=pltpu.VMEM)
    dma = pltpu.SemaphoreType.DMA
    out, over = pl.pallas_call(
        kernel,
        out_shape=(jax.ShapeDtypeStruct(slab.shape, BF16), jax.ShapeDtypeStruct((1, 1), I32)),
        in_specs=[vmem] * 3,
        out_specs=(vmem, pl.BlockSpec(memory_space=pltpu.SMEM)),
        scratch_shapes=[
            pltpu.VMEM((32, CAP, 256), BF16),
            pltpu.VMEM((16, 32, BLOCK), BF16),
            pltpu.VMEM((16, 32, BLOCK), BF16),
            pltpu.VMEM((CAP, 256), BF16),
            pltpu.VMEM((32, CAP, 256), BF16),
            pltpu.VMEM((BLOCK, BLOCK), BF16),
            dma((32,)), dma((32,)), dma((16,)), dma((16,)), dma((16,)), dma((16,)), dma((16,)), dma((16,)), dma((2,)),
            pltpu.SemaphoreType.REGULAR((16,)),
        ],
        compiler_params=pltpu.CompilerParams(collective_id=0, has_side_effects=True),
        name="lu_update",
    )(slab, jnp.transpose(panels[0]), pivots)
    return lax.cond(over[0, 0] >= CAP, general, lambda *_: out, slab, panels, pivots)


def solution(mesh):
    in_specs = (P("prow", "pcol"), P(None, "prow", "pcol"), P())
    out_specs = P("prow", "pcol")
    return jax.shard_map(local, mesh=mesh, in_specs=in_specs, out_specs=out_specs, check_vma=False)
```

time: 55.8 us -> 45.6 us (0.82)
  the two profiles are of different devices: /device:TPU:93 before, /device:TPU:8 now
where the time goes in v2:
time: 45.6 us; the launch traced here: 45.5 us
  Pallas kernels  43.9 us (96%)
  local copies, waits for them, and re-layouts  0.71 us (2%)
  between operations  0.65 us (1%)
    pallas_call x1, Pallas kernels, local(): pl.pallas_call(kernel, out_shape=(jax.ShapeDtypeStruct(slab.shape, BF16),...  43.9 us

profile of v2, /device:TPU:8, one launch (start us, length us, event | category | flops | bytes accessed | tf_op | source)
XLA Modules:
  0.0 45.5 jit_solution(9061161657425022847)
XLA Ops:
  0.0 43.9 %lu_update.1 = (bf16[512,256]{1,0:T(8,128)(2,1)S(1)}, s32[1,1]{1,0:T(1,128)}) custom-call(bf16[512,256]{1,0:T(8,128)(2,1)} %slab.1, bf16[32,512]{1,0:T(8,128)(2,1)} %bitcast.61, s32[1,512]{1,0:T(1,128)} %pivot.1), custom_call_target="tpu_custom_call" | custom-call | tf_op jit(solution)/shard_map/lu_update/pallas_call | solution.py:424
  44.5 0.2 conditional.1
  44.8 0.7 %copy.33 = bf16[512,256]{1,0:T(8,128)(2,1)} copy(bf16[512,256]{1,0:T(8,128)(2,1)S(1)} %get-tuple-element.36) | data formatting | bytes 524288

commit v3 on v2

--- a/solution.py
+++ b/solution.py
@@ -133,8 +133,10 @@
 
     partner = ((1 - y) * NZ + z, c)
 
+    across = (c + 8) % 16
+
     def peer(i):
-        return (r, (c + i) % 16)
+        return (r, (c // 8) * 8 + (c + i) % 8) if i < 8 else (r, across)
 
     def copy(src, dst, send, recv, device):
         return pltpu.make_async_remote_copy(
@@ -148,7 +150,7 @@
         pl.semaphore_signal(barrier, inc=1, device_id=device, device_id_type=MESH)
 
     hello(partner)
-    for i in range(1, 16):
+    for i in range(1, 9):
         hello(peer(i))
     for dz in near:
 
@@ -161,154 +163,197 @@
         for dz in range(5, 12):
             hello(at(dz))
 
+    pl.semaphore_wait(
+        barrier, 9 + jnp.minimum(z, 4) + jnp.maximum(z - 11, 0) + jnp.where((z > 4) & (z < 12), 1, 0)
+    )
+
+    def announce(device):
+        pl.semaphore_signal(ready.at[z], inc=1, device_id=device, device_id_type=MESH)
+
+    @pl.when((z > 4) & (z < 12))
+    def _():
+        announce((y * NZ, c))
+
+    for dz in near:
+
+        @pl.when(ring(dz) < z)
+        def _(dz=dz):
+            announce(at(dz))
+
+    def send_cand(slot, device, recv=None):
+        copy(cand.at[slot], cand.at[slot], c_send.at[0], c_recv.at[slot if recv is None else recv], device).start()
+
+    def wait_cand(slot):
+        copy(cand.at[slot], cand.at[slot], c_send.at[0], c_recv.at[slot], partner).wait_recv()
+
+    def slot_of(dz):
+        return y * NZ + ring(dz)
+
+    def send_shard(n, device):
+        copy(lbuf.at[c], lbuf.at[c], lz_send.at[n], l_recv.at[2], device).start()
+
+    def wait_shards(buf, sem, count):
+        some = buf.at[pl.ds(0, count)]
+        copy(some, some, p_send.at[0], sem, partner).wait_recv()
+
+    @pl.when(r == 0)
+    def _():
+        copy(panel, lbuf.at[c], lz_send.at[0], l_recv.at[2], partner).start()
+        lbuf[c] = panel[...]
+
     p_row = pivot[...]
     b_row = p_row // BLOCK
-    before = iota((BLOCK, BLOCK), 0) < iota((BLOCK, BLOCK), 1)
+    far_row = p_row >= BLOCK
+    before = ones(iota((BLOCK, BLOCK), 0) < iota((BLOCK, BLOCK), 1))
     in_block = iota((32, BLOCK), 0) == b_row
-    counts = dot(ones(in_block), ones(before))
+    counts = dot(ones(in_block), before)
     rank_row = jnp.sum(jnp.where(in_block, counts, 0.0), axis=0, keepdims=True).astype(I32)
-    p_col = column(p_row)
-    equal = p_col == p_row
-    later_row = jnp.max(jnp.where(equal & (iota((BLOCK, BLOCK), 0) > iota((BLOCK, BLOCK), 1)), 1, 0), axis=0, keepdims=True)
-    hit_row = jnp.max(jnp.where(p_col == iota((BLOCK, BLOCK), 1), 1, 0), axis=0, keepdims=True)
-    goes_on = ones((p_row < BLOCK) | (later_row > 0))
-    next_goes_on = dot(goes_on, ones(iota((BLOCK, BLOCK), 0) == p_row))
-    stays_row = ones((hit_row > 0) | (later_row > 0) | (next_goes_on > 0))
-    rank0_row = dot(stays_row, ones(before)).astype(I32)
-    far_row = p_row >= BLOCK
     slots = iota((CAP, BLOCK), 0)
     mine = jnp.where((b_row == r) & far_row, 1, 0) * jnp.where(rank_row == slots, 1, 0)
     local_hit = ones(iota((BLOCK, BLOCK), 0) + r * BLOCK == p_row)
-    pack = dot_nt(ones(mine > 0), local_hit)
-    pack0 = jnp.where((rank0_row == slots) & (stays_row > 0), 1.0, 0.0)
-    pack = jnp.where(r == 0, pack0, pack).astype(BF16)
-    cand[r] = dot(pack, slab[...]).astype(BF16)
-    pbuf[c] = panel[...]
-
-    @pl.when(r == 0)
-    def _():
-        lbuf[c] = panel[...]
-
-    pl.semaphore_wait(
-        barrier, 16 + jnp.minimum(z, 4) + jnp.maximum(z - 11, 0) + jnp.where((z > 4) & (z < 12), 1, 0)
-    )
-
-    def announce(device):
-        pl.semaphore_signal(ready.at[z], inc=1, device_id=device, device_id_type=MESH)
-
-    @pl.when((z > 4) & (z < 12))
-    def _():
-        announce((y * NZ, c))
+
+    def top_slots():
+        p_col = column(p_row)
+        later = (p_col == p_row) & (iota((BLOCK, BLOCK), 0) > iota((BLOCK, BLOCK), 1))
+        later_row = jnp.max(jnp.where(later, 1, 0), axis=0, keepdims=True)
+        hit_row = jnp.max(jnp.where(p_col == iota((BLOCK, BLOCK), 1), 1, 0), axis=0, keepdims=True)
+        goes_on = ones((p_row < BLOCK) | (later_row > 0))
+        next_goes_on = dot(goes_on, ones(iota((BLOCK, BLOCK), 0) == p_row))
+        stays_row = ones((hit_row > 0) | (later_row > 0) | (next_goes_on > 0))
+        return p_col, later_row, stays_row, dot(stays_row, before).astype(I32)
+
+    slot_row = jnp.where(far_row, b_row * CAP + rank_row, -1)
+
+    def chain_roots():
+        k, j = iota((BLOCK, BLOCK), 0), iota((BLOCK, BLOCK), 1)
+        parent = jnp.max(jnp.where((p_row == k) & (j < k), j, -1), axis=1, keepdims=True)
+        a = ones(jnp.where(parent >= 0, parent, iota((BLOCK, 1), 0)) == j)
+        return lax.fori_loop(0, 9, lambda _, a: dot(a, a).astype(BF16), a)
+
+    @pl.when(r > 0)
+    def _():
+        pack = dot_nt(ones(mine > 0), local_hit)
+        cand[r] = dot(pack.astype(BF16), slab[...]).astype(BF16)
+
+    @pl.when(r == 0)
+    def _():
+        _, _, stays, rank0 = top_slots()
+        cand[r] = dot(ones((rank0 == slots) & (stays > 0)), slab[...]).astype(BF16)
 
     for dz in near:
 
         @pl.when(ring(dz) < z)
         def _(dz=dz):
-            announce(at(dz))
-
-    def send_cand(n, slot, device):
-        t = copy(cand.at[slot], cand.at[slot], c_send.at[n], c_recv.at[slot], device)
-        t.start()
-
-    def wait_cand(slot):
-        copy(cand.at[slot], cand.at[slot], c_send.at[0], c_recv.at[slot], partner).wait_recv()
-
-    def slot_of(dz):
-        return y * NZ + ring(dz)
-
-    def send_shard(n, device):
-        copy(lbuf.at[c], lbuf.at[c], lz_send.at[n], l_recv.at[c], device).start()
-
-    def wait_shard(buf, sem, i):
-        copy(buf.at[i], buf.at[i], p_send.at[1], sem.at[i], partner).wait_recv()
-
-    @pl.when(r == 0)
-    def _():
-        send_shard(0, partner)
-
-    for n, dz in enumerate(near):
-
-        @pl.when(ring(dz) < z)
-        def _(n=n, dz=dz):
-            send_cand(n, r, at(dz))
-
-    send_cand(8, r, partner)
-    for i in range(1, 16):
-        copy(panel, pbuf.at[c], p_send.at[i], p_recv.at[c], peer(i)).start()
-
-    def spread_shard():
-        for i in range(1, 16):
-            copy(lbuf.at[c], lbuf.at[c], l_send.at[i], l_recv.at[c], peer(i)).start()
-
-    @pl.when((r > 0) & (z < 5))
-    def _():
-        wait_shard(lbuf, l_recv, c)
-        spread_shard()
-
-    def root_sends(steps):
+            send_cand(r, at(dz))
+
+    send_cand(r, partner, y * NZ)
+
+    def root_sends(steps, shard, slot):
         @pl.when(z == 0)
         def _():
             for dz in steps:
-                pl.semaphore_wait(ready.at[dz], 1)
-                send_shard(dz, at(dz))
-                if dz < 5 or dz > 11:
-                    send_cand(near.index(dz if dz < 5 else dz - NZ), r, at(dz))
-
-    root_sends((1, 2, 3, 4))
-
+                if slot is not None:
+                    pl.semaphore_wait(ready.at[dz], 1)
+                if slot:
+                    send_cand(r, at(dz))
+                if shard:
+                    send_shard(dz, at(dz))
+
+    @pl.when(r == NZ)
+    def _():
+        wait_shards(lbuf, l_recv.at[2], 1)
+
+    root_sends((1, 2, 3, 4), True, True)
+    root_sends((15, 14, 13, 12), False, True)
+    root_sends((5, 6, 7), True, False)
+    root_sends((11, 10, 9, 8), True, False)
+    root_sends((12, 13, 14, 15), True, None)
+
+    @pl.when(z > 4)
+    def _():
+        for dz in near:
+
+            @pl.when(ring(dz) > z)
+            def _(dz=dz):
+                pl.semaphore_wait(ready.at[ring(dz)], 1)
+                send_cand(r, at(dz))
+
+    def spread(src, buf, send, recv):
+        for i in range(8, 0, -1):
+            copy(src, buf.at[c], send.at[0], recv.at[1 if i == 8 else 0], peer(i)).start()
+
+    def spread_on(buf, send, recv):
+        wait_shards(buf, recv.at[1], 1)
+        for i in range(1, 8):
+            copy(buf.at[across], buf.at[across], send.at[0], recv.at[0], peer(i)).start()
+
+    def spread_done(buf, send, recv):
+        some = buf.at[pl.ds(0, 15)]
+        copy(some, some, send.at[0], recv.at[0], partner).wait_send()
+
+    pbuf[c] = panel[...]
+    spread(panel, pbuf, p_send, p_recv)
+
+    def spread_shard():
+        spread(lbuf.at[c], lbuf, l_send, l_recv)
+
+    @pl.when(r == NZ)
+    def _():
+        spread_shard()
+
+    @pl.when((z > 0) & (z < 5))
+    def _():
+        for dz in (1, 2, 3, 4, -1, -2, -3, -4):
+
+            @pl.when(ring(dz) > z)
+            def _(dz=dz):
+                pl.semaphore_wait(ready.at[ring(dz)], 1)
+                send_cand(r, at(dz))
+
+        wait_shards(lbuf, l_recv.at[2], 1)
+        spread_shard()
+
+    @pl.when(r == 0)
+    def _():
+        content = dot(chain_roots(), slab[...]).astype(BF16)
+        for q in range(0, 32, 4):
+            pick = ones(slot_row == iota((4 * CAP, BLOCK), 0) + q * CAP)
+            zsend[q % NZ : q % NZ + 4, q // NZ] = dot(pick, content).astype(BF16).reshape(4, CAP, 256)
+
+    p_col, later_row, stays_row, rank0_row = top_slots()
     kk = iota((BLOCK, BLOCK), 0)
     jj = iota((BLOCK, BLOCK), 1)
-    parent = jnp.max(jnp.where((p_row == kk) & (jj < kk), jj, -1), axis=1, keepdims=True)
-    k_col = iota((BLOCK, 1), 0)
-    chain = ones(jnp.where(parent >= 0, parent, k_col) == jj)
-
-    def square(times, a):
-        for _ in range(times):
-            a = dot(a, a).astype(BF16)
-        return a
-
-    for n, dz in enumerate(near):
-
-        @pl.when((z > 0) & (ring(dz) > z))
-        def _(n=n, dz=dz):
-            pl.semaphore_wait(ready.at[ring(dz)], 1)
-            send_cand(n, r, at(dz))
-
-    chain = square(4, chain)
-    root_sends((5, 15, 14, 13, 12, 6, 7, 11, 10, 9, 8))
-
-    n = 9
+
     for dz in (4, 3, 2, 1):
         wait_cand(slot_of(dz))
-        send_cand(n, slot_of(dz), at(-4))
-        n += 1
+        send_cand(slot_of(dz), at(-4))
         wait_cand(slot_of(-dz))
         if dz < 4:
-            send_cand(n, slot_of(-dz), at(4))
-            n += 1
+            send_cand(slot_of(-dz), at(4))
     for dz in near:
-        send_cand(n, slot_of(dz), partner)
-        n += 1
+        send_cand(slot_of(dz), partner, y * NZ)
+
+    spread_on(pbuf, p_send, p_recv)
+
+    def pass_on(rows):
+        return copy(rows, zbuf.at[0], z_send.at[0], z_recv.at[0], partner)
+
+    @pl.when(r == 0)
+    def _():
+        for dz in range(1, NZ):
+            copy(zsend.at[dz], zbuf, z_send.at[dz], z_recv.at[0], at(dz)).start()
+        pass_on(zsend.at[0, 1]).start()
 
     @pl.when(z > 4)
     def _():
-        wait_shard(lbuf, l_recv, c)
+        wait_shards(lbuf, l_recv.at[2], 1)
         spread_shard()
 
-    chain = square(5, chain)
-    slot_row = jnp.where(far_row, b_row * CAP + rank_row, -1)
-
-    @pl.when(r == 0)
-    def _():
-        content = dot(chain, slab[...]).astype(BF16)
-        for q in range(0, 32, 4):
-            pick = ones(slot_row == iota((4 * CAP, BLOCK), 0) + q * CAP)
-            zsend[q : q + 4] = dot(pick, content).astype(BF16).reshape(4, CAP, 256)
-
+    chain = chain_roots()
     full = jnp.max(jnp.where(far_row, rank_row, 0), axis=1, keepdims=True)
     full0 = jnp.max(jnp.where(stays_row > 0, rank0_row, 0), axis=1, keepdims=True)
     over[0, 0] = jnp.max(jnp.maximum(full, full0))
-    latest = jnp.max(jnp.where(equal & (jj < kk), jj, -1), axis=1, keepdims=True)
+    latest = jnp.max(jnp.where((p_col == p_row) & (jj < kk), jj, -1), axis=1, keepdims=True)
     source = dot(ones(latest == jj), chain) + jnp.where((latest < 0) & (p_col == jj), 1.0, 0.0)
     rank0_col = column(jnp.where(stays_row > 0, rank0_row, -1))
     near_pick = dot(source.astype(BF16), ones(rank0_col == iota((BLOCK, CAP), 1)))
@@ -316,31 +361,20 @@
     far_pick = ones((slot_col == iota((BLOCK, 32 * CAP), 1)) & (latest < 0))
     pick = jnp.concatenate([near_pick.astype(BF16), far_pick[:, CAP:]], axis=1)
 
-    def other_ring():
-        half = zsend.at[pl.ds(NZ, NZ)]
-        return copy(half, half, z_send.at[0], z_recv.at[1], partner)
-
-    @pl.when(r == 0)
-    def _():
-        other_ring().start()
-
-    @pl.when(r == NZ)
-    def _():
-        other_ring().wait_recv()
-        zbuf[...] = zsend[NZ]
-
-    @pl.when(z == 0)
-    def _():
-        for dz in range(1, NZ):
-            copy(zsend.at[y * NZ + dz], zbuf, z_send.at[dz], z_recv.at[0], at(dz)).start()
+    @pl.when(r > 0)
+    def _():
+        spread_on(lbuf, l_send, l_recv)
 
     for dz in (5, 6, 7, 8, -5, -6, -7):
         wait_cand(slot_of(dz))
-        send_cand(n, slot_of(dz), partner)
-        n += 1
-
-    for i in range(1, 16):
-        wait_shard(pbuf, p_recv, (c + i) % 16)
+        send_cand(slot_of(dz), partner, y * NZ)
+
+    @pl.when((y == 0) & (z > 0))
+    def _():
+        copy(zbuf, zbuf, z_send.at[0], z_recv.at[0], partner).wait_recv()
+        pass_on(zbuf.at[1]).start()
+
+    wait_shards(pbuf, p_recv.at[0], 14)
 
     @pl.when(r == 0)
     def _():
@@ -354,8 +388,7 @@
 
     @pl.when(r > 0)
     def _():
-        for i in range(1, 16):
-            wait_shard(lbuf, l_recv, (c + i) % 16)
+        wait_shards(lbuf, l_recv.at[0], 14)
 
     diagonal_t = lbuf[...].reshape(BLOCK, BLOCK)
 
@@ -369,8 +402,8 @@
     first_high, first_low = split(first)
     second_high, second_low = split(second)
 
-    for dz in range(NZ):
-        wait_cand((1 - y) * NZ + dz)
+    theirs = cand.at[pl.ds((1 - y) * NZ, NZ)]
+    copy(theirs, theirs, c_send.at[0], c_recv.at[(1 - y) * NZ], partner).wait_recv()
     top = dot(pick, cand[...].reshape(32 * CAP, 256))
     half = top[:256].astype(BF16)
     upper1 = dot(first_high, half) + dot(first_low, half)
@@ -381,13 +414,13 @@
 
     @pl.when(r > 0)
     def _():
-        @pl.when(z > 0)
+        @pl.when(y == 1)
         def _():
-            copy(zbuf, zbuf, z_send.at[0], z_recv.at[0], partner).wait_recv()
+            pass_on(zbuf.at[1]).wait_recv()
 
         last = jnp.where(later_row > 0, 0, mine)
         place = dot_nt(local_hit, ones(last > 0))
-        moved = dot(place.astype(BF16), zbuf[...])
+        moved = dot(place.astype(BF16), zbuf[0])
         hit = jnp.sum(place, axis=1, keepdims=True) > 0
         product = dot(straight[...], upper)
         out[...] = (jnp.where(hit, moved, slab[...].astype(F32)) - product).astype(BF16)
@@ -396,26 +429,28 @@
     def _():
         out[...] = upper
 
-    for i in range(31):
-        copy(cand.at[r], cand.at[r], c_send.at[i], c_recv.at[r], partner).wait_send()
-    for i in range(1, 16):
-        copy(panel, pbuf.at[c], p_send.at[i], p_recv.at[c], peer(i)).wait_send()
+    every = cand.at[pl.ds(0, 31)]
+    copy(every, every, c_send.at[0], c_recv.at[0], partner).wait_send()
+    spread_done(pbuf, p_send, p_recv)
 
     @pl.when(r > 0)
     def _():
-        for i in range(1, 16):
-            copy(lbuf.at[c], lbuf.at[c], l_send.at[i], l_recv.at[c], peer(i)).wait_send()
+        spread_done(lbuf, l_send, l_recv)
 
     @pl.when(z == 0)
     def _():
         for dz in range(1, NZ):
             copy(lbuf.at[c], lbuf.at[c], lz_send.at[dz], l_recv.at[c], partner).wait_send()
-            copy(zsend.at[dz], zbuf, z_send.at[dz], z_recv.at[0], partner).wait_send()
 
     @pl.when(r == 0)
     def _():
         copy(lbuf.at[c], lbuf.at[c], lz_send.at[0], l_recv.at[c], partner).wait_send()
-        other_ring().wait_send()
+        for dz in range(1, NZ):
+            copy(zsend.at[dz], zbuf, z_send.at[dz], z_recv.at[0], at(dz)).wait_send()
+
+    @pl.when(y == 0)
+    def _():
+        pass_on(zbuf.at[1]).wait_send()
 
 
 def local(slab, panels, pivots):
@@ -430,8 +465,8 @@
             pltpu.VMEM((32, CAP, 256), BF16),
             pltpu.VMEM((16, 32, BLOCK), BF16),
             pltpu.VMEM((16, 32, BLOCK), BF16),
-            pltpu.VMEM((CAP, 256), BF16),
-            pltpu.VMEM((32, CAP, 256), BF16),
+            pltpu.VMEM((2, CAP, 256), BF16),
+            pltpu.VMEM((NZ, 2, CAP, 256), BF16),
             pltpu.VMEM((BLOCK, BLOCK), BF16),
             dma((32,)), dma((32,)), dma((16,)), dma((16,)), dma((16,)), dma((16,)), dma((16,)), dma((16,)), dma((2,)),
             pltpu.SemaphoreType.REGULAR((16,)),

time: 45.6 us -> 42.8 us (0.939)
  the two profiles are of different devices: /device:TPU:8 before, /device:TPU:489 now
where the time goes in v3:
time: 42.8 us; the launch traced here: 42.6 us
  Pallas kernels  41.1 us (96%)
  local copies, waits for them, and re-layouts  0.71 us (2%)
  between operations  0.65 us (2%)
    pallas_call x1, Pallas kernels, local(): pl.pallas_call(kernel, out_shape=(jax.ShapeDtypeStruct(slab.shape, BF16),...  41.1 us

profile of v3, /device:TPU:489, one launch (start us, length us, event | category | flops | bytes accessed | tf_op | source)
XLA Modules:
  0.0 42.6 jit_solution(2357130350181244033)
XLA Ops:
  0.0 41.1 %lu_update.1 = (bf16[512,256]{1,0:T(8,128)(2,1)S(1)}, s32[1,1]{1,0:T(1,128)}) custom-call(bf16[512,256]{1,0:T(8,128)(2,1)} %slab.1, bf16[32,512]{1,0:T(8,128)(2,1)} %bitcast.61, s32[1,512]{1,0:T(1,128)} %pivot.1), custom_call_target="tpu_custom_call" | custom-call | tf_op jit(solution)/shard_map/lu_update/pallas_call | solution.py:459
  41.7 0.2 conditional.1
  41.9 0.7 %copy.33 = bf16[512,256]{1,0:T(8,128)(2,1)} copy(bf16[512,256]{1,0:T(8,128)(2,1)S(1)} %get-tuple-element.36) | data formatting | bytes 524288

commit v4 on v3

--- a/solution.py
+++ b/solution.py
@@ -170,7 +170,7 @@
     def announce(device):
         pl.semaphore_signal(ready.at[z], inc=1, device_id=device, device_id_type=MESH)
 
-    @pl.when((z > 4) & (z < 12))
+    @pl.when((z > 4) & (z < 12) & (z != 9) & (z != 10))
     def _():
         announce((y * NZ, c))
 
@@ -266,7 +266,7 @@
     root_sends((1, 2, 3, 4), True, True)
     root_sends((15, 14, 13, 12), False, True)
     root_sends((5, 6, 7), True, False)
-    root_sends((11, 10, 9, 8), True, False)
+    root_sends((11, 8), True, False)
     root_sends((12, 13, 14, 15), True, None)
 
     @pl.when(z > 4)
@@ -347,6 +347,12 @@
     @pl.when(z > 4)
     def _():
         wait_shards(lbuf, l_recv.at[2], 1)
+
+        @pl.when(z == 8)
+        def _():
+            send_shard(1, at(1))
+            send_shard(2, at(2))
+
         spread_shard()
 
     chain = chain_roots()
@@ -439,7 +445,12 @@
 
     @pl.when(z == 0)
     def _():
-        for dz in range(1, NZ):
+        for dz in (1, 2, 3, 4, 5, 6, 7, 8, 11, 12, 13, 14, 15):
+            copy(lbuf.at[c], lbuf.at[c], lz_send.at[dz], l_recv.at[c], partner).wait_send()
+
+    @pl.when(z == 8)
+    def _():
+        for dz in (1, 2):
             copy(lbuf.at[c], lbuf.at[c], lz_send.at[dz], l_recv.at[c], partner).wait_send()
 
     @pl.when(r == 0)

time: 42.8 us -> 41.7 us (0.974)
  the two profiles are of different devices: /device:TPU:489 before, /device:TPU:345 now
where the time goes in v4:
time: 41.7 us; the launch traced here: 41.6 us
  Pallas kernels  40 us (96%)
  local copies, waits for them, and re-layouts  0.71 us (2%)
  between operations  0.65 us (2%)
    pallas_call x1, Pallas kernels, local(): pl.pallas_call(kernel, out_shape=(jax.ShapeDtypeStruct(slab.shape, BF16),...  40 us

profile of v4, /device:TPU:345, one launch (start us, length us, event | category | flops | bytes accessed | tf_op | source)
XLA Modules:
  0.0 41.6 jit_solution(909331344333984292)
XLA Ops:
  0.0 40.0 %lu_update.1 = (bf16[512,256]{1,0:T(8,128)(2,1)S(1)}, s32[1,1]{1,0:T(1,128)}) custom-call(bf16[512,256]{1,0:T(8,128)(2,1)} %slab.1, bf16[32,512]{1,0:T(8,128)(2,1)} %bitcast.61, s32[1,512]{1,0:T(1,128)} %pivot.1), custom_call_target="tpu_custom_call" | custom-call | tf_op jit(solution)/shard_map/lu_update/pallas_call | solution.py:470
  40.7 0.2 conditional.1
  40.9 0.7 %copy.33 = bf16[512,256]{1,0:T(8,128)(2,1)} copy(bf16[512,256]{1,0:T(8,128)(2,1)S(1)} %get-tuple-element.36) | data formatting | bytes 524288

commit v5 on v4

--- a/solution.py
+++ b/solution.py
@@ -170,7 +170,7 @@
     def announce(device):
         pl.semaphore_signal(ready.at[z], inc=1, device_id=device, device_id_type=MESH)
 
-    @pl.when((z > 4) & (z < 12) & (z != 9) & (z != 10))
+    @pl.when((z > 4) & (z < 9))
     def _():
         announce((y * NZ, c))
 
@@ -266,7 +266,7 @@
     root_sends((1, 2, 3, 4), True, True)
     root_sends((15, 14, 13, 12), False, True)
     root_sends((5, 6, 7), True, False)
-    root_sends((11, 8), True, False)
+    root_sends((8,), True, False)
     root_sends((12, 13, 14, 15), True, None)
 
     @pl.when(z > 4)
@@ -352,6 +352,7 @@
         def _():
             send_shard(1, at(1))
             send_shard(2, at(2))
+            send_shard(3, at(3))
 
         spread_shard()
 
@@ -445,12 +446,12 @@
 
     @pl.when(z == 0)
     def _():
-        for dz in (1, 2, 3, 4, 5, 6, 7, 8, 11, 12, 13, 14, 15):
+        for dz in (1, 2, 3, 4, 5, 6, 7, 8, 12, 13, 14, 15):
             copy(lbuf.at[c], lbuf.at[c], lz_send.at[dz], l_recv.at[c], partner).wait_send()
 
     @pl.when(z == 8)
     def _():
-        for dz in (1, 2):
+        for dz in (1, 2, 3):
             copy(lbuf.at[c], lbuf.at[c], lz_send.at[dz], l_recv.at[c], partner).wait_send()
 
     @pl.when(r == 0)

time: 41.7 us -> 42.6 us (1.022)
  the two profiles are of different devices: /device:TPU:345 before, /device:TPU:353 now
where the time goes in v5:
time: 42.6 us; the launch traced here: 42.5 us
  Pallas kernels  40.9 us (96%)
  local copies, waits for them, and re-layouts  0.71 us (2%)
  between operations  0.65 us (2%)
    pallas_call x1, Pallas kernels, local(): pl.pallas_call(kernel, out_shape=(jax.ShapeDtypeStruct(slab.shape, BF16),...  40.9 us

profile of v5, /device:TPU:353, one launch (start us, length us, event | category | flops | bytes accessed | tf_op | source)
XLA Modules:
  0.0 42.5 jit_solution(13197895956209463238)
XLA Ops:
  0.0 40.9 %lu_update.1 = (bf16[512,256]{1,0:T(8,128)(2,1)S(1)}, s32[1,1]{1,0:T(1,128)}) custom-call(bf16[512,256]{1,0:T(8,128)(2,1)} %slab.1, bf16[32,512]{1,0:T(8,128)(2,1)} %bitcast.61, s32[1,512]{1,0:T(1,128)} %pivot.1), custom_call_target="tpu_custom_call" | custom-call | tf_op jit(solution)/shard_map/lu_update/pallas_call | solution.py:471
  41.6 0.2 conditional.1
  41.8 0.7 %copy.33 = bf16[512,256]{1,0:T(8,128)(2,1)} copy(bf16[512,256]{1,0:T(8,128)(2,1)S(1)} %get-tuple-element.36) | data formatting | bytes 524288
